TPU v7x, 32 devices: a whole 2x2x4 slice. The times are simulated.
32 devices in a mesh: grp: 2 (over y), band: 4 (over z), sub: 2 (over x), kern: 2 (over core).
Axes of the slice: x: 2, y: 2, z: 4, core: 2. Of those that a mesh axis runs over, the one named last changes fastest.
Arguments:
- screens: bfloat16 [32, 2, 64, 64], P('band'), may hold values from -6 to 6
- visibilities: bfloat16 [1024, 2, 128], P(('grp', 'band', 'sub', 'kern')), parts along dimension 0, may hold values from -6 to 6
- vis_columns: int32 [1024, 128], P(('grp', 'band', 'sub', 'kern')), parts along dimension 0, may hold values from 0 to 63
- band_route: int32 [1024, 1], P(('grp', 'band', 'sub', 'kern')), parts along dimension 0, may hold values from 0 to 3; in each aligned block of 32 rows (0 to 31, 32 to 63, ...) at most 16 rows name the same one
- screen_choice: int32 [1024], P(('grp', 'band', 'sub', 'kern')), parts along dimension 0, may hold values from 0 to 31
- offsets: int32 [1024, 2], P(('grp', 'band', 'sub', 'kern')), parts along dimension 0, may hold values from 0 to 7
- row_cell: int32 [1024], P(('grp', 'band', 'sub', 'kern')), parts along dimension 0, may hold values from 0 to 192
- col_cell: int32 [1024], P(('grp', 'band', 'sub', 'kern')), parts along dimension 0, may hold values from 0 to 896
Outputs:
- grid: float32 [2, 2048, 1024], P(None, ('grp', 'band', 'sub', 'kern')), parts along dimension 1
There are 2 independent parts, one for each index of `grp`. A program takes and returns all parts, laid end to end along the dimension named above; an argument that names none is the same for every part. Nothing has to cross between parts.
Inputs may be any that keep to these rules, and one draw needn't show every extreme that they name: `band_route`: among the blocks of one device no band is named more than 16 times, a bound that some block reaches.
All inputs are finite; a program needn't handle non-finite values.
Results may differ from a plain program's by a relative error of at most 0.0058.
Values may be sent and summed in bfloat16 or wider, within the bound.
No kernel may reach another device: no remote copies, remote signals or barrier semaphores. Data moves between devices by JAX's collectives and lax.ppermute only.
A program may use at most 64 MiB of HBM per device.

v0:
```python
import functools
import math

import jax
import jax.numpy as jnp
import numpy as np
from jax import lax
from jax.experimental import pallas as pl
from jax.experimental.pallas import tpu as pltpu
from jax.sharding import PartitionSpec as P


OVERS = 8
BR = 256
NCOL = 1024
LANES = 128
FIELDS = 8
UNROLL = 60
DIRECT_MOST = 4
VMEM_GRANT = 24 * 1024 * 1024

f32, bf16, i32 = jnp.float32, jnp.bfloat16, jnp.int32


def dft_tables(support):
    centred = np.arange(support, dtype=np.float32) - np.float32(support // 2)
    fractions = np.arange(OVERS, dtype=np.float32) / np.float32(OVERS)
    frequency = centred[None, :, None] + fractions[:, None, None]
    phases = np.float32(-2.0 * math.pi) * frequency * centred[None, None, :] / np.float32(support)
    scale = np.float32(support)
    return (
        (np.cos(phases) / scale).astype(jnp.bfloat16).astype(np.float32),
        (np.sin(phases) / scale).astype(jnp.bfloat16).astype(np.float32),
    )


def table_constants(support, rows):
    real, imag = dft_tables(support)
    padded = np.zeros((OVERS, support + 2 * rows, 2 * support), np.float32)
    padded[:, rows : rows + support] = np.concatenate([real, imag], axis=2)
    top = np.concatenate([real, -imag], axis=2)
    low = np.concatenate([imag, real], axis=2)
    columns = np.concatenate([top, low], axis=1).astype(jnp.bfloat16)
    return padded.reshape(-1, 2 * support), columns


def in_hbm(array):
    return pltpu.with_memory_space_constraint(array, pltpu.HBM)


def iota(shape, axis):
    return lax.broadcasted_iota(i32, shape, axis)


def nt_dot(left, right):
    return lax.dot_general(left, right, (((1,), (1,)), ((), ())), preferred_element_type=f32)


def nn_dot(left, right):
    return jnp.dot(left, right, preferred_element_type=f32)


def send_kernel(
    band_count, splits, capacity, direct,
    *refs,
):
    sources, outs, held = refs[:8], refs[8:-10], refs[-10:-2]
    line_ref, sems = refs[-2:]
    share, _, support, _ = held[0].shape
    first = lax.axis_index("kern") * share if splits > 1 else 0
    copies = []
    for index in (3, 4, 5, 6, 7, 2, 1, 0):
        source = sources[index].at[pl.ds(first, share)] if index == 0 else sources[index]
        copies.append(pltpu.make_async_copy(source, held[index], sems.at[index]))
    for copy in copies:
        copy.start()
    screens, values, columns, route, choice, offsets, row_cell, col_cell = held
    blocks, width = columns.shape
    me = lax.axis_index("band")
    for copy in copies[:5]:
        copy.wait()
    target = route[...]
    slots = band_count * capacity
    match = (iota((band_count, blocks), 0) == target).astype(f32)
    earlier = (iota((blocks, blocks), 0) < iota((blocks, blocks), 1)).astype(f32).astype(bf16)
    before = nn_dot(match.astype(bf16), earlier)
    rank = jnp.sum(before * match, axis=0, keepdims=True).astype(i32)
    slot = target * capacity + rank
    pick = (iota((slots, blocks), 0) == slot).astype(f32).astype(bf16)
    column = col_cell[...]
    fields = [
        choice[...], offsets[pl.ds(0, 1), :], offsets[pl.ds(1, 1), :], row_cell[...],
        column // LANES, column % LANES, jnp.ones_like(column), jnp.zeros_like(column),
    ]
    field_at = iota((FIELDS, blocks), 0)
    table = jnp.zeros((FIELDS, blocks), i32)
    for index, field in enumerate(fields):
        table = jnp.where(field_at == index, field, table)
    spread = (iota((FIELDS, LANES), 0) == iota((FIELDS, LANES), 1)).astype(f32).astype(bf16)
    meta = nt_dot(pick, table.astype(f32).astype(bf16)).astype(bf16)
    for copy in copies[5:]:
        copy.wait()
    for block in range(blocks):
        hits = iota((support, width), 0) == columns[pl.ds(block, 1), :]
        line = nt_dot(values[block], hits.astype(f32).astype(bf16))
        line_ref[0, pl.ds(block, 1), :] = line[0:1]
        line_ref[1, pl.ds(block, 1), :] = line[1:2]
    at_row, at_lane = iota((support, LANES), 0), iota((support, LANES), 1)
    place_re = (at_lane == (LANES - at_row) % LANES).astype(f32).astype(bf16)
    place_im = (at_lane == support - at_row).astype(f32).astype(bf16)
    lines = nn_dot(line_ref[0].astype(bf16), place_re) + nn_dot(line_ref[1].astype(bf16), place_im)
    payload = jnp.concatenate(
        [nn_dot(pick, lines.astype(bf16)), nn_dot(meta, spread)], axis=1
    )
    slot_ref = outs[-1]
    slot_ref[...] = payload
    outs = outs[:-1] if direct else [outs[0].at[step] for step in range(band_count)]
    for step, out in enumerate(outs):
        dest = partner(me, step, band_count) if direct else step
        mine = slot_ref[pl.ds(dest * capacity, capacity), :]
        out[pl.ds(0, capacity), :] = mine[:, :LANES].astype(bf16)
        out[pl.ds(capacity, capacity), :] = mine[:, LANES:].astype(bf16)
    for index in range(share):
        both = jnp.concatenate(
            [screens[index, 0].astype(f32), screens[index, 1].astype(f32)], axis=1
        ).astype(bf16)
        for out in outs:
            out[pl.ds(2 * capacity + index * support, support), :] = both


def partner(me, step, count):
    if count & (count - 1) == 0:
        return me ^ step
    return lax.rem(me + step, count)


def grid_kernel(
    band_count, kern_count, splits, held, deep, per_band, rows, support, direct, parts_of, *refs
):
    pieces, screen_parts = refs[: parts_of[0]], refs[parts_of[0] : parts_of[1]]
    row_tables, column_tables, out = refs[parts_of[1] : parts_of[1] + 3]
    screen_ref, line_ref, meta_vmem, meta_smem, total, half_ref, kernel_ref, skew_ref, stage, sem, sems = (
        refs[parts_of[1] + 3 :]
    )
    share = per_band // splits
    slices = [(piece, at) for piece in pieces for at in range(piece.shape[0])]
    lines = jnp.concatenate([piece[at, :held, :] for piece, at in slices], axis=0)
    metas = jnp.concatenate([piece[at, held : 2 * held, :] for piece, at in slices], axis=0)
    count = lines.shape[0]
    spread = (iota((FIELDS, LANES), 0) == iota((FIELDS, LANES), 1)).astype(f32).astype(bf16)
    fields = nt_dot(spread, metas)
    kern = lax.axis_index("kern")
    low = ((lax.axis_index("sub") * kern_count + kern) * rows).astype(f32)
    row_at = fields[3:4]
    live = (fields[6:7] > 0.5) & (row_at < low + rows) & (row_at + support > low)
    live = live.astype(f32)
    upper = (iota((count, count), 0) < iota((count, count), 1)).astype(f32).astype(bf16)
    rank = nn_dot(jnp.broadcast_to(live, (FIELDS, count)).astype(bf16), upper)[0:1]
    start = (low + rows - row_at) * live
    field_at = iota((FIELDS, count), 0)
    packed = jnp.where(field_at == 3, start, fields) * live
    pick = (iota((count, count), 0).astype(f32) == rank).astype(f32) * live
    pick = pick.astype(bf16)
    line_ref[pl.ds(0, count), :] = nn_dot(pick, lines)
    line_ref[pl.ds(count, LANES), :] = jnp.zeros((LANES, LANES), f32)
    chosen = nt_dot(packed.astype(bf16), pick)
    number = jnp.sum(live)
    screen = chosen[0:1].astype(i32)
    sizes = [screen_ref.shape[0] // (2 * support), row_tables.shape[0], OVERS]
    bits = [(size - 1).bit_length() for size in sizes]
    shifts = [sum(bits[: at + 1]) for at in range(3)]
    assert shifts[-1] + (NCOL - 1).bit_length() < 32
    me = lax.axis_index("band")
    band_of = screen // per_band
    if not direct:
        step_of = band_of
    elif band_count & (band_count - 1) == 0:
        step_of = band_of ^ me
    else:
        step_of = (band_of - me + band_count) % band_count
    within = screen % per_band
    place = step_of * share + within % share
    if splits > 1:
        place = place + ((within // share) != kern).astype(i32) * (band_count * share)
    table_row = chosen[1:2].astype(i32) * (support + 2 * rows) + chosen[3:4].astype(i32)
    col = chosen[4:5].astype(i32) * LANES + chosen[5:6].astype(i32)
    word = place
    for shift, field in zip(shifts, (table_row, chosen[2:3].astype(i32), col)):
        word = word + field * (1 << shift)
    meta_vmem[:, pl.ds(0, count)] = word
    meta_vmem[:, pl.ds(count, LANES)] = jnp.broadcast_to(number.astype(i32), (1, LANES))
    copy = pltpu.make_async_copy(meta_vmem, meta_smem, sem)
    copy.start()
    lane = iota((support, LANES), 1)
    sign = jnp.where(lane < support, -1.0, 1.0).astype(f32)
    span = NCOL // band_count

    def unfold(step, carry):
        for part_at, part in enumerate(screen_parts):
            for index in range(share):
                both = part[step, pl.ds(deep + index * support, support), :]
                turned = pltpu.roll(both.astype(f32), support, 1) * sign
                at = ((part_at * band_count + step) * share + index) * 2 * support
                at = pl.multiple_of(at, 2 * support)
                screen_ref[pl.ds(at, support), :] = both
                screen_ref[pl.ds(at + support, support), :] = turned.astype(bf16)
        total[pl.ds(pl.multiple_of(step * span, span), span), :] = jnp.zeros((span, 2 * rows), f32)
        return carry

    lax.fori_loop(0, band_count, unfold, 0)
    y_at, l_at = iota((2 * support, LANES), 0), iota((2 * support, LANES), 1)
    lag = y_at - l_at % support
    keep = ((lag >= 0) & (lag < support)).astype(f32).astype(bf16)
    wide = 2 * support
    copy.wait()

    def part_of(word, at):
        lower = shifts[at - 1] if at else 0
        high = word >> lower
        return high & ((1 << bits[at]) - 1) if at < 3 else high

    def turn(index, carry):
        ids = [index * UNROLL + extra for extra in range(UNROLL)]
        words = [meta_smem[0, k] for k in ids]
        for at, word in enumerate(words):
            left = row_tables[pl.ds(part_of(word, 1), rows), :].astype(bf16)
            screen_at = pl.multiple_of(part_of(word, 0) * wide, wide)
            right = screen_ref[pl.ds(screen_at, wide), :]
            half_ref[at] = nn_dot(left, right).astype(bf16)
        for at, k in enumerate(ids):
            line = jnp.broadcast_to(line_ref[pl.ds(k, 1), :], (wide, LANES))
            skew_ref[at] = pltpu.roll(line, 0, 1, stride=1, stride_axis=0).astype(bf16) * keep
        for at, word in enumerate(words):
            both = nt_dot(column_tables[part_of(word, 2)], half_ref[at]).astype(bf16)
            real, imag = both[:support], both[support:]
            kernel_ref[at, pl.ds(0, support), :] = jnp.concatenate([real, imag], axis=1)
            kernel_ref[at, pl.ds(support, support), :] = jnp.concatenate([-imag, real], axis=1)
        for at, word in enumerate(words):
            window = pl.ds(part_of(word, 3), wide)
            total[window, :] = total[window, :] + nn_dot(skew_ref[at], kernel_ref[at])
        return carry

    turns = (meta_smem[0, count] + (UNROLL - 1)) // UNROLL
    lax.fori_loop(0, turns, turn, 0)
    writes = []
    for at in range(NCOL // LANES):
        turned = total[pl.ds(at * LANES, LANES), :].T
        stage[at, 0] = turned[:rows]
        stage[at, 1] = turned[rows:]
        target = out.at[:, :, pl.ds(at * LANES, LANES)]
        writes.append(pltpu.make_async_copy(stage.at[at], target, sems.at[at]))
        writes[-1].start()
    for write in writes:
        write.wait()


def table_kernel(row_source, column_source, row_tables, column_tables, sems):
    copies = [
        pltpu.make_async_copy(row_source, row_tables, sems.at[0]),
        pltpu.make_async_copy(column_source, column_tables, sems.at[1]),
    ]
    for copy in copies:
        copy.start()
    for copy in copies:
        copy.wait()


def exchange(parts, axis, count):
    if count & (count - 1) == 0:
        perms = [[(i, i ^ step) for i in range(count)] for step in range(count)]
    else:
        perms = [[((i + step) % count, i) for i in range(count)] for step in range(count)]
    return [parts[0]] + [lax.ppermute(parts[step], axis, perms[step]) for step in range(1, count)]


def program(
    screens, visibilities, vis_columns, band_route, screen_choice, offsets, row_cell, col_cell
):
    band_count = lax.axis_size("band")
    sub_count, kern_count = lax.axis_size("sub"), lax.axis_size("kern")
    per_band, _, support, _ = screens.shape
    blocks = visibilities.shape[0]
    capacity = 2 * blocks // band_count
    rows = BR // (sub_count * kern_count)
    members = sub_count * kern_count
    group = ("sub", "kern")
    direct = band_count <= DIRECT_MOST and members in (1, 2, 4)
    splits = 2 if kern_count == 2 and per_band % 2 == 0 else 1
    share = per_band // splits
    depth = 2 * capacity + share * support
    vmem = pl.BlockSpec(memory_space=pltpu.VMEM)
    hbm = pl.BlockSpec(memory_space=pltpu.HBM)
    grant = pltpu.CompilerParams(vmem_limit_bytes=VMEM_GRANT)
    if direct:
        messages = [jax.ShapeDtypeStruct((depth, LANES), bf16)] * band_count
    else:
        messages = [jax.ShapeDtypeStruct((band_count, depth, LANES), bf16)]
    sent = pl.pallas_call(
        functools.partial(send_kernel, band_count, splits, capacity, direct),
        out_shape=messages + [jax.ShapeDtypeStruct((band_count * capacity, 2 * LANES), f32)],
        in_specs=[hbm] * 8,
        out_specs=[vmem] * (len(messages) + 1),
        scratch_shapes=[
            pltpu.VMEM((share,) + screens.shape[1:], bf16),
            pltpu.VMEM(visibilities.shape, bf16),
            pltpu.VMEM(vis_columns.shape, i32),
            pltpu.VMEM((1, blocks), i32),
            pltpu.VMEM((1, blocks), i32),
            pltpu.VMEM((2, blocks), i32),
            pltpu.VMEM((1, blocks), i32),
            pltpu.VMEM((1, blocks), i32),
            pltpu.VMEM((2, blocks, support), f32),
            pltpu.SemaphoreType.DMA((8,)),
        ],
        compiler_params=grant,
    )(
        *map(
            in_hbm,
            (
                screens, visibilities, vis_columns, band_route.reshape(1, blocks),
                screen_choice.reshape(1, blocks), offsets.T, row_cell.reshape(1, blocks),
                col_cell.reshape(1, blocks),
            ),
        )
    )
    count = members * band_count * capacity
    if direct:
        own = jnp.stack(exchange(sent[:-1], "band", band_count))
        slots = own[:, : 2 * capacity]
        pieces, screen_parts, held, deep = [own], [own], capacity, 2 * capacity
        for step in range(1, members):
            whole = splits > 1 and step == 1
            perm = [(i, i ^ step) for i in range(members)]
            got = lax.ppermute(own if whole else slots, group, perm)
            pieces.append(got)
            if whole:
                screen_parts.append(got)
    else:
        own = lax.all_to_all(sent[0], "band", 0, 0, tiled=True)
        slots = lax.all_gather(own[:, : 2 * capacity], group, axis=0, tiled=True)
        slots = slots.reshape(members * band_count, 2, capacity, LANES)
        pieces = [slots.transpose(1, 0, 2, 3).reshape(1, 2 * count, LANES)]
        screen_parts, held, deep = [own[:, 2 * capacity :]], count, 0
        if splits > 1:
            perm = [(i, i ^ 1) for i in range(kern_count)]
            screen_parts.append(lax.ppermute(screen_parts[0], "kern", perm))
    tables = [jnp.asarray(table) for table in table_constants(support, rows)]
    tables = pl.pallas_call(
        table_kernel,
        out_shape=[jax.ShapeDtypeStruct(table.shape, table.dtype) for table in tables],
        in_specs=[hbm] * 2,
        out_specs=[vmem] * 2,
        scratch_shapes=[pltpu.SemaphoreType.DMA((2,))],
        compiler_params=grant,
        cost_estimate=pl.CostEstimate(flops=0, bytes_accessed=1 << 21, transcendentals=0),
    )(*map(in_hbm, tables))
    parts_of = (len(pieces), len(pieces) + len(screen_parts))
    return pl.pallas_call(
        functools.partial(
            grid_kernel, band_count, kern_count, splits, held, deep, per_band, rows, support,
            direct, parts_of,
        ),
        out_shape=jax.ShapeDtypeStruct((2, rows, NCOL), f32),
        in_specs=[vmem] * (parts_of[1] + 2),
        out_specs=hbm,
        scratch_shapes=[
            pltpu.VMEM((per_band * band_count * 2 * support, LANES), bf16),
            pltpu.VMEM((count + LANES, LANES), f32),
            pltpu.VMEM((1, count + LANES), i32),
            pltpu.SMEM((1, count + LANES), i32),
            pltpu.VMEM((NCOL, 2 * rows), f32),
            pltpu.VMEM((UNROLL, rows, 2 * support), bf16),
            pltpu.VMEM((UNROLL, 2 * support, 2 * rows), bf16),
            pltpu.VMEM((UNROLL, 2 * support, 2 * support), bf16),
            pltpu.VMEM((NCOL // LANES, 2, rows, LANES), f32),
            pltpu.SemaphoreType.DMA(()),
            pltpu.SemaphoreType.DMA((NCOL // LANES,)),
        ],
        compiler_params=grant,
    )(*pieces, *screen_parts, *tables)


def solution(mesh):
    in_specs = (
        P("band", None, None, None),
        P(("grp", "band", "sub", "kern"), None, None),
        P(("grp", "band", "sub", "kern"), None),
        P(("grp", "band", "sub", "kern"), None),
        P(("grp", "band", "sub", "kern")),
        P(("grp", "band", "sub", "kern"), None),
        P(("grp", "band", "sub", "kern")),
        P(("grp", "band", "sub", "kern")),
    )
    out_specs = P(None, ("grp", "band", "sub", "kern"), None)
    return jax.shard_map(program, mesh=mesh, in_specs=in_specs, out_specs=out_specs, check_vma=False)
```

profile of v0, /device:TPU:17, one launch (start us, length us, event | category | flops | bytes accessed | tf_op | source)
XLA Modules:
  0.0 24.6 jit_solution(13832098893633927928)
XLA Ops:
  0.0 2.4 %shard_map.100 = (bf16[288,128]{1,0:T(8,128)(2,1)S(1)}, bf16[288,128]{1,0:T(8,128)(2,1)S(1)}, bf16[288,128]{1,0:T(8,128)(2,1)S(1)}, bf16[288,128]{1,0:T(8,128)(2,1)S(1)}, f32[64,256]{1,0:T(8,128)}) custom-call(bf16[8,2,64,64]{3,2,1,0:T(8,128)(2,1)} %refs_0_.1, bf16[32,2,128]{2,1,0:T(2,128)(2,1)} %refs_1_.1, s32[32,128]{1,0:T(8,128)} %refs_2_.1, ...), custom_call_target="tpu_custom_call" | custom-call | tf_op jit(solution)/shard_map/pallas_call | solution.py:298
  2.4 1.4 %collective-permute-start = (bf16[288,128]{1,0:T(8,128)(2,1)S(1)}, bf16[288,128]{1,0:T(8,128)(2,1)S(1)}, u32[]{:S(2)}, u32[]{:S(2)}) collective-permute-start(bf16[288,128]{1,0:T(8,128)(2,1)S(1)} %get-tuple-element.12), channel_id=1, source_target_pairs={{0,4},{4,0},{8,12},{12,8},{1,5},{5,1},{9,13},{13,9},{2,6},{6,2},{1... | collective-permute-start | bytes 221192 | tf_op jit(solution)/shard_map/ppermute | solution.py:273
  3.7 0.1 collective-permute-start.1
  3.8 1.3 %collective-permute-start.2 = (bf16[288,128]{1,0:T(8,128)(2,1)S(1)}, bf16[288,128]{1,0:T(8,128)(2,1)S(1)}, u32[]{:S(2)}, u32[]{:S(2)}) collective-permute-start(bf16[288,128]{1,0:T(8,128)(2,1)S(1)} %get-tuple-element.14), channel_id=1, source_target_pairs={{0,12},{4,8},{8,4},{12,0},{1,13},{5,9},{9,5},{13,1},{2,14},{6,10},... | collective-permute-start | bytes 221192 | tf_op jit(solution)/shard_map/ppermute | solution.py:273
  5.1 0.6 %collective-permute-done = bf16[288,128]{1,0:T(8,128)(2,1)S(1)} collective-permute-done((bf16[288,128]{1,0:T(8,128)(2,1)S(1)}, bf16[288,128]{1,0:T(8,128)(2,1)S(1)}, u32[]{:S(2)}, u32[]{:S(2)}) %collective-permute-start) | collective-permute-done | bytes 73760 | tf_op jit(solution)/shard_map/ppermute | solution.py:273
  5.6 2.3 %collective-permute-done.1 = bf16[288,128]{1,0:T(8,128)(2,1)S(1)} collective-permute-done((bf16[288,128]{1,0:T(8,128)(2,1)S(1)}, bf16[288,128]{1,0:T(8,128)(2,1)S(1)}, u32[]{:S(2)}, u32[]{:S(2)}) %collective-permute-start.1) | collective-permute-done | bytes 73760 | tf_op jit(solution)/shard_map/ppermute | solution.py:273
  7.9 3.3 %collective-permute-done.2 = bf16[288,128]{1,0:T(8,128)(2,1)S(1)} collective-permute-done((bf16[288,128]{1,0:T(8,128)(2,1)S(1)}, bf16[288,128]{1,0:T(8,128)(2,1)S(1)}, u32[]{:S(2)}, u32[]{:S(2)}) %collective-permute-start.2) | collective-permute-done | bytes 73760 | tf_op jit(solution)/shard_map/ppermute | solution.py:273
  11.3 1.9 %collective-permute-start.3 = (bf16[4,288,128]{2,1,0:T(8,128)(2,1)S(1)}, bf16[4,288,128]{2,1,0:T(8,128)(2,1)S(1)}, u32[]{:S(2)}, u32[]{:S(2)}) collective-permute-start(bf16[4,288,128]{2,1,0:T(8,128)(2,1)S(1)} %pad_maximum_fusion.refs_0_.refs_4_), channel_id=1, source_target_pairs={{0,1},{1,0},{2,3},{3,2},{4,5},{5,4},{6,7},{7,6},{8,9},{9,8},{10,11... | collective-permute-start | bytes 884744 | tf_op jit(solution)/shard_map/ppermute | solution.py:334
  13.2 1.2 %collective-permute-start.5 = (bf16[4,32,128]{2,1,0:T(8,128)(2,1)S(1)}, bf16[4,32,128]{2,1,0:T(8,128)(2,1)S(1)}, u32[]{:S(2)}, u32[]{:S(2)}) collective-permute-start(bf16[4,32,128]{2,1,0:T(8,128)(2,1)S(1)} %slice.4), channel_id=1, source_target_pairs={{0,3},{1,2},{2,1},{3,0},{4,7},{5,6},{6,5},{7,4},{8,11},{9,10},{10,... | collective-permute-start | bytes 98312 | tf_op jit(solution)/shard_map/ppermute | solution.py:334
  14.3 0.3 %collective-permute-start.4 = (bf16[4,32,128]{2,1,0:T(8,128)(2,1)S(1)}, bf16[4,32,128]{2,1,0:T(8,128)(2,1)S(1)}, u32[]{:S(2)}, u32[]{:S(2)}) collective-permute-start(bf16[4,32,128]{2,1,0:T(8,128)(2,1)S(1)} %slice.4), channel_id=1, source_target_pairs={{0,2},{1,3},{2,0},{3,1},{4,6},{5,7},{6,4},{7,5},{8,10},{9,11},{10,... | collective-permute-start | bytes 98312 | tf_op jit(solution)/shard_map/ppermute | solution.py:334
  14.6 1.2 %shard_map.101 = (f32[1536,128]{1,0:T(8,128)S(1)}, bf16[8,128,128]{2,1,0:T(8,128)(2,1)S(1)}) custom-call(f32[1536,128]{1,0:T(8,128)} %constant.4.clone.row_source, bf16[8,128,128]{2,1,0:T(8,128)(2,1)} %constant.5.clone.column_source), custom_call_target="tpu_custom_call" | custom-call | bytes 2097152 | tf_op jit(solution)/shard_map/pallas_call | solution.py:348
  15.8 0.7 %collective-permute-done.5.refs_3_ = bf16[4,32,128]{2,1,0:T(8,128)(2,1)S(1)} collective-permute-done((bf16[4,32,128]{2,1,0:T(8,128)(2,1)S(1)}, bf16[4,32,128]{2,1,0:T(8,128)(2,1)S(1)}, u32[]{:S(2)}, u32[]{:S(2)}) %collective-permute-start.5) | collective-permute-done | bytes 32800 | tf_op jit(solution)/shard_map/ppermute | solution.py:334
  16.5 0.6 %collective-permute-done.4.refs_2_ = bf16[4,32,128]{2,1,0:T(8,128)(2,1)S(1)} collective-permute-done((bf16[4,32,128]{2,1,0:T(8,128)(2,1)S(1)}, bf16[4,32,128]{2,1,0:T(8,128)(2,1)S(1)}, u32[]{:S(2)}, u32[]{:S(2)}) %collective-permute-start.4) | collective-permute-done | bytes 32800 | tf_op jit(solution)/shard_map/ppermute | solution.py:334
  17.1 0.0 collective-permute-done.3.refs_1_.refs_5_
  17.1 7.5 %shard_map.102 = f32[2,64,1024]{2,1,0:T(8,128)} custom-call(bf16[4,288,128]{2,1,0:T(8,128)(2,1)S(1)} %pad_maximum_fusion.refs_0_.refs_4_, bf16[4,288,128]{2,1,0:T(8,128)(2,1)S(1)} %collective-permute-done.3.refs_1_.refs_5_, bf16[4,32,128]{2,1,0:T(8,128)(2,1)S(1)} %collective-permute-done.4.refs_2_, bf16[4,32,128]{2,1,0:T(8,128)(2,1)S(1)} %collective-permute-done.5.refs_3_, ...), custom_call_target="tpu_custom_call" | custom-call | tf_op jit(solution)/shard_map/pallas_call | solution.py:358
  (2 shorter events, 0.0 us)
Async XLA Ops:
  2.4 3.3 %collective-permute-start = (bf16[288,128]{1,0:T(8,128)(2,1)S(1)}, bf16[288,128]{1,0:T(8,128)(2,1)S(1)}, u32[]{:S(2)}, u32[]{:S(2)}) collective-permute-start(bf16[288,128]{1,0:T(8,128)(2,1)S(1)} %get-tuple-element.12), channel_id=1, source_target_pairs={{0,4},{4,0},{8,12},{12,8},{1,5},{5,1},{9,13},{13,9},{2,6},{6,2},{1... | collective-permute-start | bytes 221192 | tf_op jit(solution)/shard_map/ppermute | solution.py:273
  3.7 4.2 %collective-permute-start.1 = (bf16[288,128]{1,0:T(8,128)(2,1)S(1)}, bf16[288,128]{1,0:T(8,128)(2,1)S(1)}, u32[]{:S(2)}, u32[]{:S(2)}) collective-permute-start(bf16[288,128]{1,0:T(8,128)(2,1)S(1)} %get-tuple-element.13), channel_id=1, source_target_pairs={{0,8},{4,12},{8,0},{12,4},{1,9},{5,13},{9,1},{13,5},{2,10},{6,14},... | collective-permute-start | bytes 221192 | tf_op jit(solution)/shard_map/ppermute | solution.py:273
  3.8 7.4 %collective-permute-start.2 = (bf16[288,128]{1,0:T(8,128)(2,1)S(1)}, bf16[288,128]{1,0:T(8,128)(2,1)S(1)}, u32[]{:S(2)}, u32[]{:S(2)}) collective-permute-start(bf16[288,128]{1,0:T(8,128)(2,1)S(1)} %get-tuple-element.14), channel_id=1, source_target_pairs={{0,12},{4,8},{8,4},{12,0},{1,13},{5,9},{9,5},{13,1},{2,14},{6,10},... | collective-permute-start | bytes 221192 | tf_op jit(solution)/shard_map/ppermute | solution.py:273
  11.3 5.8 %collective-permute-start.3 = (bf16[4,288,128]{2,1,0:T(8,128)(2,1)S(1)}, bf16[4,288,128]{2,1,0:T(8,128)(2,1)S(1)}, u32[]{:S(2)}, u32[]{:S(2)}) collective-permute-start(bf16[4,288,128]{2,1,0:T(8,128)(2,1)S(1)} %pad_maximum_fusion.refs_0_.refs_4_), channel_id=1, source_target_pairs={{0,1},{1,0},{2,3},{3,2},{4,5},{5,4},{6,7},{7,6},{8,9},{9,8},{10,11... | collective-permute-start | bytes 884744 | tf_op jit(solution)/shard_map/ppermute | solution.py:334
  13.2 3.3 %collective-permute-start.5 = (bf16[4,32,128]{2,1,0:T(8,128)(2,1)S(1)}, bf16[4,32,128]{2,1,0:T(8,128)(2,1)S(1)}, u32[]{:S(2)}, u32[]{:S(2)}) collective-permute-start(bf16[4,32,128]{2,1,0:T(8,128)(2,1)S(1)} %slice.4), channel_id=1, source_target_pairs={{0,3},{1,2},{2,1},{3,0},{4,7},{5,6},{6,5},{7,4},{8,11},{9,10},{10,... | collective-permute-start | bytes 98312 | tf_op jit(solution)/shard_map/ppermute | solution.py:334
  14.3 2.8 %collective-permute-start.4 = (bf16[4,32,128]{2,1,0:T(8,128)(2,1)S(1)}, bf16[4,32,128]{2,1,0:T(8,128)(2,1)S(1)}, u32[]{:S(2)}, u32[]{:S(2)}) collective-permute-start(bf16[4,32,128]{2,1,0:T(8,128)(2,1)S(1)} %slice.4), channel_id=1, source_target_pairs={{0,2},{1,3},{2,0},{3,1},{4,6},{5,7},{6,4},{7,5},{8,10},{9,11},{10,... | collective-permute-start | bytes 98312 | tf_op jit(solution)/shard_map/ppermute | solution.py:334
where the time goes:
time: 24.8 us; the launch traced here: 24.6 us
  Pallas kernels  11.1 us (45%)
  waiting for transfers between devices  7.45 us (30%)
  starting transfers between devices  6.02 us (24%)
    pallas_call x1, Pallas kernels, program(): pl.pallas_call(functools.partial(grid_kernel, band_count, kern_count, spl...  7.49 us
    ppermute x3, waiting for transfers between devices, exchange(): lax.ppermute(parts[step], axis, perms[step])  6.15 us
    ppermute x3, starting transfers between devices, program(): got = lax.ppermute(own if whole else slots, group, perm)  3.31 us
    ppermute x3, starting transfers between devices, exchange(): lax.ppermute(parts[step], axis, perms[step])  2.71 us
    pallas_call x1, Pallas kernels, program(): pl.pallas_call(functools.partial(send_kernel, band_count, splits, capacit...  2.37 us
    ppermute x3, waiting for transfers between devices, program(): got = lax.ppermute(own if whole else slots, group, perm)  1.3 us
    pallas_call x1, Pallas kernels, program(): pl.pallas_call(table_kernel, out_shape=[jax.ShapeDtypeStruct(table.shape,...  1.2 us
  transfers between devices with their start and end apart: 6, of which 5 were waited for; matrix products, arithmetic and copies ran while one was open for 0% of the time, Pallas kernels for 5%

commit v1 on v0

--- a/solution.py
+++ b/solution.py
@@ -61,11 +61,11 @@
 
 
 def send_kernel(
-    band_count, splits, capacity, direct,
+    band_count, splits, capacity, fold, direct,
     *refs,
 ):
-    sources, outs, held = refs[:8], refs[8:-10], refs[-10:-2]
-    line_ref, sems = refs[-2:]
+    sources, outs, held = refs[:8], refs[8:-11], refs[-11:-3]
+    line_ref, slot_ref, sems = refs[-3:]
     share, _, support, _ = held[0].shape
     first = lax.axis_index("kern") * share if splits > 1 else 0
     copies = []
@@ -112,20 +112,23 @@
     payload = jnp.concatenate(
         [nn_dot(pick, lines.astype(bf16)), nn_dot(meta, spread)], axis=1
     )
-    slot_ref = outs[-1]
     slot_ref[...] = payload
-    outs = outs[:-1] if direct else [outs[0].at[step] for step in range(band_count)]
+    outs = outs if direct else [outs[0].at[step] for step in range(band_count)]
     for step, out in enumerate(outs):
         dest = partner(me, step, band_count) if direct else step
         mine = slot_ref[pl.ds(dest * capacity, capacity), :]
         out[pl.ds(0, capacity), :] = mine[:, :LANES].astype(bf16)
-        out[pl.ds(capacity, capacity), :] = mine[:, LANES:].astype(bf16)
+        part = capacity // fold
+        metas = mine[:part, LANES:]
+        if fold > 1:
+            metas = metas + pltpu.roll(mine[part:, LANES:], LANES // 2, 1)
+        out[pl.ds(capacity, part), :] = metas.astype(bf16)
     for index in range(share):
         both = jnp.concatenate(
             [screens[index, 0].astype(f32), screens[index, 1].astype(f32)], axis=1
         ).astype(bf16)
         for out in outs:
-            out[pl.ds(2 * capacity + index * support, support), :] = both
+            out[pl.ds(capacity + capacity // fold + index * support, support), :] = both
 
 
 def partner(me, step, count):
@@ -135,7 +138,7 @@
 
 
 def grid_kernel(
-    band_count, kern_count, splits, held, deep, per_band, rows, support, direct, parts_of, *refs
+    band_count, kern_count, splits, held, fold, deep, per_band, rows, support, direct, parts_of, *refs
 ):
     pieces, screen_parts = refs[: parts_of[0]], refs[parts_of[0] : parts_of[1]]
     row_tables, column_tables, out = refs[parts_of[1] : parts_of[1] + 3]
@@ -144,11 +147,16 @@
     )
     share = per_band // splits
     slices = [(piece, at) for piece in pieces for at in range(piece.shape[0])]
-    lines = jnp.concatenate([piece[at, :held, :] for piece, at in slices], axis=0)
-    metas = jnp.concatenate([piece[at, held : 2 * held, :] for piece, at in slices], axis=0)
+    part = held // fold
+    lines = jnp.concatenate(
+        [piece[at, turn * part : (turn + 1) * part, :] for turn in range(fold) for piece, at in slices],
+        axis=0,
+    )
+    metas = jnp.concatenate([piece[at, held : held + part, :] for piece, at in slices], axis=0)
     count = lines.shape[0]
-    spread = (iota((FIELDS, LANES), 0) == iota((FIELDS, LANES), 1)).astype(f32).astype(bf16)
-    fields = nt_dot(spread, metas)
+    f_at, f_lane = iota((FIELDS, LANES), 0), iota((FIELDS, LANES), 1)
+    spreads = [(f_lane == f_at + turn * (LANES // 2)).astype(f32).astype(bf16) for turn in range(fold)]
+    fields = jnp.concatenate([nt_dot(spread, metas) for spread in spreads], axis=1)
     kern = lax.axis_index("kern")
     low = ((lax.axis_index("sub") * kern_count + kern) * rows).astype(f32)
     row_at = fields[3:4]
@@ -287,7 +295,9 @@
     direct = band_count <= DIRECT_MOST and members in (1, 2, 4)
     splits = 2 if kern_count == 2 and per_band % 2 == 0 else 1
     share = per_band // splits
-    depth = 2 * capacity + share * support
+    fold = 2 if direct and capacity % 16 == 0 else 1
+    top = capacity + capacity // fold
+    depth = top + share * support
     vmem = pl.BlockSpec(memory_space=pltpu.VMEM)
     hbm = pl.BlockSpec(memory_space=pltpu.HBM)
     grant = pltpu.CompilerParams(vmem_limit_bytes=VMEM_GRANT)
@@ -296,10 +306,10 @@
     else:
         messages = [jax.ShapeDtypeStruct((band_count, depth, LANES), bf16)]
     sent = pl.pallas_call(
-        functools.partial(send_kernel, band_count, splits, capacity, direct),
-        out_shape=messages + [jax.ShapeDtypeStruct((band_count * capacity, 2 * LANES), f32)],
+        functools.partial(send_kernel, band_count, splits, capacity, fold, direct),
+        out_shape=messages,
         in_specs=[hbm] * 8,
-        out_specs=[vmem] * (len(messages) + 1),
+        out_specs=[vmem] * len(messages),
         scratch_shapes=[
             pltpu.VMEM((share,) + screens.shape[1:], bf16),
             pltpu.VMEM(visibilities.shape, bf16),
@@ -310,6 +320,7 @@
             pltpu.VMEM((1, blocks), i32),
             pltpu.VMEM((1, blocks), i32),
             pltpu.VMEM((2, blocks, support), f32),
+            pltpu.VMEM((band_count * capacity, 2 * LANES), f32),
             pltpu.SemaphoreType.DMA((8,)),
         ],
         compiler_params=grant,
@@ -325,9 +336,9 @@
     )
     count = members * band_count * capacity
     if direct:
-        own = jnp.stack(exchange(sent[:-1], "band", band_count))
-        slots = own[:, : 2 * capacity]
-        pieces, screen_parts, held, deep = [own], [own], capacity, 2 * capacity
+        own = jnp.stack(exchange(sent, "band", band_count))
+        slots = own[:, :top]
+        pieces, screen_parts, held, deep = [own], [own], capacity, top
         for step in range(1, members):
             whole = splits > 1 and step == 1
             perm = [(i, i ^ step) for i in range(members)]
@@ -357,7 +368,7 @@
     parts_of = (len(pieces), len(pieces) + len(screen_parts))
     return pl.pallas_call(
         functools.partial(
-            grid_kernel, band_count, kern_count, splits, held, deep, per_band, rows, support,
+            grid_kernel, band_count, kern_count, splits, held, fold, deep, per_band, rows, support,
             direct, parts_of,
         ),
         out_shape=jax.ShapeDtypeStruct((2, rows, NCOL), f32),

time: 24.8 us -> 24 us (0.968)
  Pallas kernels: 11.1 us -> 10.5 us
  waiting for transfers between devices: 7.45 us -> 7.19 us
    pallas_call x1, Pallas kernels: 2.37 us -> 1.82 us  [program(): pl.pallas_call(functools.partial(send_kernel, band_count, splits, capacit...]
where the time goes in v1:
time: 24 us; the launch traced here: 23.8 us
  Pallas kernels  10.5 us (44%)
  waiting for transfers between devices  7.19 us (30%)
  starting transfers between devices  6.02 us (25%)
    pallas_call x1, Pallas kernels, program(): pl.pallas_call(functools.partial(grid_kernel, band_count, kern_count, spl...  7.52 us
    ppermute x3, waiting for transfers between devices, exchange(): lax.ppermute(parts[step], axis, perms[step])  5.98 us
    ppermute x3, starting transfers between devices, program(): got = lax.ppermute(own if whole else slots, group, perm)  3.31 us
    ppermute x3, starting transfers between devices, exchange(): lax.ppermute(parts[step], axis, perms[step])  2.71 us
    pallas_call x1, Pallas kernels, program(): pl.pallas_call(functools.partial(send_kernel, band_count, splits, capacit...  1.82 us
    ppermute x3, waiting for transfers between devices, program(): got = lax.ppermute(own if whole else slots, group, perm)  1.21 us
    pallas_call x1, Pallas kernels, program(): pl.pallas_call(table_kernel, out_shape=[jax.ShapeDtypeStruct(table.shape,...  1.2 us
  transfers between devices with their start and end apart: 6, of which 5 were waited for; matrix products, arithmetic and copies ran while one was open for 0% of the time, Pallas kernels for 5%

profile of v1, /device:TPU:17, one launch (start us, length us, event | category | flops | bytes accessed | tf_op | source)
XLA Modules:
  0.0 23.8 jit_solution(6466004448983711098)
XLA Ops:
  0.0 1.8 %shard_map.100 = (bf16[280,128]{1,0:T(8,128)(2,1)S(1)}, bf16[280,128]{1,0:T(8,128)(2,1)S(1)}, bf16[280,128]{1,0:T(8,128)(2,1)S(1)}, bf16[280,128]{1,0:T(8,128)(2,1)S(1)}) custom-call(bf16[8,2,64,64]{3,2,1,0:T(8,128)(2,1)} %refs_0_.1, bf16[32,2,128]{2,1,0:T(2,128)(2,1)} %refs_1_.1, s32[32,128]{1,0:T(8,128)} %refs_2_.1, s32[1,32]{1,0:T(1,128)} %bitcast.14, ...), custom_call_target="tpu_custom_call" | custom-call | tf_op jit(solution)/shard_map/pallas_call | solution.py:308
  1.8 1.4 %collective-permute-start = (bf16[280,128]{1,0:T(8,128)(2,1)S(1)}, bf16[280,128]{1,0:T(8,128)(2,1)S(1)}, u32[]{:S(2)}, u32[]{:S(2)}) collective-permute-start(bf16[280,128]{1,0:T(8,128)(2,1)S(1)} %get-tuple-element.12), channel_id=1, source_target_pairs={{0,4},{4,0},{8,12},{12,8},{1,5},{5,1},{9,13},{13,9},{2,6},{6,2},{1... | collective-permute-start | bytes 215048 | tf_op jit(solution)/shard_map/ppermute | solution.py:281
  3.2 0.1 collective-permute-start.1
  3.2 1.3 %collective-permute-start.2 = (bf16[280,128]{1,0:T(8,128)(2,1)S(1)}, bf16[280,128]{1,0:T(8,128)(2,1)S(1)}, u32[]{:S(2)}, u32[]{:S(2)}) collective-permute-start(bf16[280,128]{1,0:T(8,128)(2,1)S(1)} %get-tuple-element.14), channel_id=1, source_target_pairs={{0,12},{4,8},{8,4},{12,0},{1,13},{5,9},{9,5},{13,1},{2,14},{6,10},... | collective-permute-start | bytes 215048 | tf_op jit(solution)/shard_map/ppermute | solution.py:281
  4.5 0.5 %collective-permute-done = bf16[280,128]{1,0:T(8,128)(2,1)S(1)} collective-permute-done((bf16[280,128]{1,0:T(8,128)(2,1)S(1)}, bf16[280,128]{1,0:T(8,128)(2,1)S(1)}, u32[]{:S(2)}, u32[]{:S(2)}) %collective-permute-start) | collective-permute-done | bytes 71712 | tf_op jit(solution)/shard_map/ppermute | solution.py:281
  5.1 2.3 %collective-permute-done.1 = bf16[280,128]{1,0:T(8,128)(2,1)S(1)} collective-permute-done((bf16[280,128]{1,0:T(8,128)(2,1)S(1)}, bf16[280,128]{1,0:T(8,128)(2,1)S(1)}, u32[]{:S(2)}, u32[]{:S(2)}) %collective-permute-start.1) | collective-permute-done | bytes 71712 | tf_op jit(solution)/shard_map/ppermute | solution.py:281
  7.4 3.1 %collective-permute-done.2 = bf16[280,128]{1,0:T(8,128)(2,1)S(1)} collective-permute-done((bf16[280,128]{1,0:T(8,128)(2,1)S(1)}, bf16[280,128]{1,0:T(8,128)(2,1)S(1)}, u32[]{:S(2)}, u32[]{:S(2)}) %collective-permute-start.2) | collective-permute-done | bytes 71712 | tf_op jit(solution)/shard_map/ppermute | solution.py:281
  10.6 1.9 %collective-permute-start.3 = (bf16[4,280,128]{2,1,0:T(8,128)(2,1)S(1)}, bf16[4,280,128]{2,1,0:T(8,128)(2,1)S(1)}, u32[]{:S(2)}, u32[]{:S(2)}) collective-permute-start(bf16[4,280,128]{2,1,0:T(8,128)(2,1)S(1)} %pad_maximum_fusion.refs_0_.refs_4_), channel_id=1, source_target_pairs={{0,1},{1,0},{2,3},{3,2},{4,5},{5,4},{6,7},{7,6},{8,9},{9,8},{10,11... | collective-permute-start | bytes 860168 | tf_op jit(solution)/shard_map/ppermute | solution.py:345
  12.4 1.2 %collective-permute-start.5 = (bf16[4,24,128]{2,1,0:T(8,128)(2,1)S(1)}, bf16[4,24,128]{2,1,0:T(8,128)(2,1)S(1)}, u32[]{:S(2)}, u32[]{:S(2)}) collective-permute-start(bf16[4,24,128]{2,1,0:T(8,128)(2,1)S(1)} %slice.4), channel_id=1, source_target_pairs={{0,3},{1,2},{2,1},{3,0},{4,7},{5,6},{6,5},{7,4},{8,11},{9,10},{10,... | collective-permute-start | bytes 73736 | tf_op jit(solution)/shard_map/ppermute | solution.py:345
  13.6 0.3 %collective-permute-start.4 = (bf16[4,24,128]{2,1,0:T(8,128)(2,1)S(1)}, bf16[4,24,128]{2,1,0:T(8,128)(2,1)S(1)}, u32[]{:S(2)}, u32[]{:S(2)}) collective-permute-start(bf16[4,24,128]{2,1,0:T(8,128)(2,1)S(1)} %slice.4), channel_id=1, source_target_pairs={{0,2},{1,3},{2,0},{3,1},{4,6},{5,7},{6,4},{7,5},{8,10},{9,11},{10,... | collective-permute-start | bytes 73736 | tf_op jit(solution)/shard_map/ppermute | solution.py:345
  13.9 1.2 %shard_map.101 = (f32[1536,128]{1,0:T(8,128)S(1)}, bf16[8,128,128]{2,1,0:T(8,128)(2,1)S(1)}) custom-call(f32[1536,128]{1,0:T(8,128)} %constant.4.clone.row_source, bf16[8,128,128]{2,1,0:T(8,128)(2,1)} %constant.5.clone.column_source), custom_call_target="tpu_custom_call" | custom-call | bytes 2097152 | tf_op jit(solution)/shard_map/pallas_call | solution.py:359
  15.1 0.6 %collective-permute-done.5.refs_3_ = bf16[4,24,128]{2,1,0:T(8,128)(2,1)S(1)} collective-permute-done((bf16[4,24,128]{2,1,0:T(8,128)(2,1)S(1)}, bf16[4,24,128]{2,1,0:T(8,128)(2,1)S(1)}, u32[]{:S(2)}, u32[]{:S(2)}) %collective-permute-start.5) | collective-permute-done | bytes 24608 | tf_op jit(solution)/shard_map/ppermute | solution.py:345
  15.7 0.6 %collective-permute-done.4.refs_2_ = bf16[4,24,128]{2,1,0:T(8,128)(2,1)S(1)} collective-permute-done((bf16[4,24,128]{2,1,0:T(8,128)(2,1)S(1)}, bf16[4,24,128]{2,1,0:T(8,128)(2,1)S(1)}, u32[]{:S(2)}, u32[]{:S(2)}) %collective-permute-start.4) | collective-permute-done | bytes 24608 | tf_op jit(solution)/shard_map/ppermute | solution.py:345
  16.3 0.0 collective-permute-done.3.refs_1_.refs_5_
  16.3 7.5 %shard_map.102 = f32[2,64,1024]{2,1,0:T(8,128)} custom-call(bf16[4,280,128]{2,1,0:T(8,128)(2,1)S(1)} %pad_maximum_fusion.refs_0_.refs_4_, bf16[4,280,128]{2,1,0:T(8,128)(2,1)S(1)} %collective-permute-done.3.refs_1_.refs_5_, bf16[4,24,128]{2,1,0:T(8,128)(2,1)S(1)} %collective-permute-done.4.refs_2_, bf16[4,24,128]{2,1,0:T(8,128)(2,1)S(1)} %collective-permute-done.5.refs_3_, ...), custom_call_target="tpu_custom_call" | custom-call | tf_op jit(solution)/shard_map/pallas_call | solution.py:369
  (2 shorter events, 0.0 us)
Async XLA Ops:
  1.8 3.2 %collective-permute-start = (bf16[280,128]{1,0:T(8,128)(2,1)S(1)}, bf16[280,128]{1,0:T(8,128)(2,1)S(1)}, u32[]{:S(2)}, u32[]{:S(2)}) collective-permute-start(bf16[280,128]{1,0:T(8,128)(2,1)S(1)} %get-tuple-element.12), channel_id=1, source_target_pairs={{0,4},{4,0},{8,12},{12,8},{1,5},{5,1},{9,13},{13,9},{2,6},{6,2},{1... | collective-permute-start | bytes 215048 | tf_op jit(solution)/shard_map/ppermute | solution.py:281
  3.2 4.2 %collective-permute-start.1 = (bf16[280,128]{1,0:T(8,128)(2,1)S(1)}, bf16[280,128]{1,0:T(8,128)(2,1)S(1)}, u32[]{:S(2)}, u32[]{:S(2)}) collective-permute-start(bf16[280,128]{1,0:T(8,128)(2,1)S(1)} %get-tuple-element.13), channel_id=1, source_target_pairs={{0,8},{4,12},{8,0},{12,4},{1,9},{5,13},{9,1},{13,5},{2,10},{6,14},... | collective-permute-start | bytes 215048 | tf_op jit(solution)/shard_map/ppermute | solution.py:281
  3.2 7.3 %collective-permute-start.2 = (bf16[280,128]{1,0:T(8,128)(2,1)S(1)}, bf16[280,128]{1,0:T(8,128)(2,1)S(1)}, u32[]{:S(2)}, u32[]{:S(2)}) collective-permute-start(bf16[280,128]{1,0:T(8,128)(2,1)S(1)} %get-tuple-element.14), channel_id=1, source_target_pairs={{0,12},{4,8},{8,4},{12,0},{1,13},{5,9},{9,5},{13,1},{2,14},{6,10},... | collective-permute-start | bytes 215048 | tf_op jit(solution)/shard_map/ppermute | solution.py:281
  10.6 5.7 %collective-permute-start.3 = (bf16[4,280,128]{2,1,0:T(8,128)(2,1)S(1)}, bf16[4,280,128]{2,1,0:T(8,128)(2,1)S(1)}, u32[]{:S(2)}, u32[]{:S(2)}) collective-permute-start(bf16[4,280,128]{2,1,0:T(8,128)(2,1)S(1)} %pad_maximum_fusion.refs_0_.refs_4_), channel_id=1, source_target_pairs={{0,1},{1,0},{2,3},{3,2},{4,5},{5,4},{6,7},{7,6},{8,9},{9,8},{10,11... | collective-permute-start | bytes 860168 | tf_op jit(solution)/shard_map/ppermute | solution.py:345
  12.4 3.3 %collective-permute-start.5 = (bf16[4,24,128]{2,1,0:T(8,128)(2,1)S(1)}, bf16[4,24,128]{2,1,0:T(8,128)(2,1)S(1)}, u32[]{:S(2)}, u32[]{:S(2)}) collective-permute-start(bf16[4,24,128]{2,1,0:T(8,128)(2,1)S(1)} %slice.4), channel_id=1, source_target_pairs={{0,3},{1,2},{2,1},{3,0},{4,7},{5,6},{6,5},{7,4},{8,11},{9,10},{10,... | collective-permute-start | bytes 73736 | tf_op jit(solution)/shard_map/ppermute | solution.py:345
  13.6 2.7 %collective-permute-start.4 = (bf16[4,24,128]{2,1,0:T(8,128)(2,1)S(1)}, bf16[4,24,128]{2,1,0:T(8,128)(2,1)S(1)}, u32[]{:S(2)}, u32[]{:S(2)}) collective-permute-start(bf16[4,24,128]{2,1,0:T(8,128)(2,1)S(1)} %slice.4), channel_id=1, source_target_pairs={{0,2},{1,3},{2,0},{3,1},{4,6},{5,7},{6,4},{7,5},{8,10},{9,11},{10,... | collective-permute-start | bytes 73736 | tf_op jit(solution)/shard_map/ppermute | solution.py:345

commit v2 on v1

--- a/solution.py
+++ b/solution.py
@@ -16,6 +16,7 @@
 LANES = 128
 FIELDS = 8
 UNROLL = 60
+LAST_TURN = 48
 DIRECT_MOST = 4
 VMEM_GRANT = 24 * 1024 * 1024
 
@@ -227,8 +228,8 @@
         high = word >> lower
         return high & ((1 << bits[at]) - 1) if at < 3 else high
 
-    def turn(index, carry):
-        ids = [index * UNROLL + extra for extra in range(UNROLL)]
+    def turn(base, size, index, carry):
+        ids = [base + index * size + extra for extra in range(size)]
         words = [meta_smem[0, k] for k in ids]
         for at, word in enumerate(words):
             left = row_tables[pl.ds(part_of(word, 1), rows), :].astype(bf16)
@@ -248,8 +249,13 @@
             total[window, :] = total[window, :] + nn_dot(skew_ref[at], kernel_ref[at])
         return carry
 
-    turns = (meta_smem[0, count] + (UNROLL - 1)) // UNROLL
-    lax.fori_loop(0, turns, turn, 0)
+    pieces_here = meta_smem[0, count]
+    full = pieces_here // UNROLL
+    left_over = pieces_here - full * UNROLL
+    full = full + (left_over > LAST_TURN).astype(i32)
+    lax.fori_loop(0, full, functools.partial(turn, 0, UNROLL), 0)
+    short = ((left_over > 0) & (left_over <= LAST_TURN)).astype(i32)
+    lax.fori_loop(0, short, functools.partial(turn, full * UNROLL, LAST_TURN), 0)
     writes = []
     for at in range(NCOL // LANES):
         turned = total[pl.ds(at * LANES, LANES), :].T

time: 24 us -> 23.7 us (0.987)
  the two profiles are of different devices: /device:TPU:17 before, /device:TPU:0 now
where the time goes in v2:
time: 23.7 us; the launch traced here: 23.2 us
  waiting for transfers between devices  8.3 us (35%)
  starting transfers between devices  7.9 us (33%)
  Pallas kernels  6.91 us (29%)
    ppermute x3, waiting for transfers between devices, exchange(): lax.ppermute(parts[step], axis, perms[step])  6.22 us
    ppermute x3, starting transfers between devices, exchange(): lax.ppermute(parts[step], axis, perms[step])  5.71 us
    pallas_call x1, Pallas kernels, program(): pl.pallas_call(functools.partial(grid_kernel, band_count, kern_count, spl...  3.89 us
    ppermute x3, starting transfers between devices, program(): got = lax.ppermute(own if whole else slots, group, perm)  2.19 us
    ppermute x3, waiting for transfers between devices, program(): got = lax.ppermute(own if whole else slots, group, perm)  2.08 us
    pallas_call x1, Pallas kernels, program(): pl.pallas_call(functools.partial(send_kernel, band_count, splits, capacit...  1.82 us
    pallas_call x1, Pallas kernels, program(): pl.pallas_call(table_kernel, out_shape=[jax.ShapeDtypeStruct(table.shape,...  1.2 us
  transfers between devices with their start and end apart: 6, of which 3 were waited for; matrix products, arithmetic and copies ran while one was open for 0% of the time, Pallas kernels for 5%

profile of v2, /device:TPU:0, one launch (start us, length us, event | category | flops | bytes accessed | tf_op | source)
XLA Modules:
  0.0 23.2 jit_solution(6330846546447195225)
XLA Ops:
  0.0 1.8 %shard_map.100 = (bf16[280,128]{1,0:T(8,128)(2,1)S(1)}, bf16[280,128]{1,0:T(8,128)(2,1)S(1)}, bf16[280,128]{1,0:T(8,128)(2,1)S(1)}, bf16[280,128]{1,0:T(8,128)(2,1)S(1)}) custom-call(bf16[8,2,64,64]{3,2,1,0:T(8,128)(2,1)} %refs_0_.1, bf16[32,2,128]{2,1,0:T(2,128)(2,1)} %refs_1_.1, s32[32,128]{1,0:T(8,128)} %refs_2_.1, s32[1,32]{1,0:T(1,128)} %bitcast.14, ...), custom_call_target="tpu_custom_call" | custom-call | tf_op jit(solution)/shard_map/pallas_call | solution.py:314
  1.8 3.1 %collective-permute-start = (bf16[280,128]{1,0:T(8,128)(2,1)S(1)}, bf16[280,128]{1,0:T(8,128)(2,1)S(1)}, u32[]{:S(2)}, u32[]{:S(2)}) collective-permute-start(bf16[280,128]{1,0:T(8,128)(2,1)S(1)} %get-tuple-element.12), channel_id=1, source_target_pairs={{0,4},{4,0},{8,12},{12,8},{1,5},{5,1},{9,13},{13,9},{2,6},{6,2},{1... | collective-permute-start | bytes 215048 | tf_op jit(solution)/shard_map/ppermute | solution.py:287
  4.9 2.6 %collective-permute-start.1 = (bf16[280,128]{1,0:T(8,128)(2,1)S(1)}, bf16[280,128]{1,0:T(8,128)(2,1)S(1)}, u32[]{:S(2)}, u32[]{:S(2)}) collective-permute-start(bf16[280,128]{1,0:T(8,128)(2,1)S(1)} %get-tuple-element.13), channel_id=1, source_target_pairs={{0,8},{4,12},{8,0},{12,4},{1,9},{5,13},{9,1},{13,5},{2,10},{6,14},... | collective-permute-start | bytes 215048 | tf_op jit(solution)/shard_map/ppermute | solution.py:287
  7.5 0.0 collective-permute-start.2
  7.5 0.0 collective-permute-done
  7.5 5.1 %collective-permute-done.1 = bf16[280,128]{1,0:T(8,128)(2,1)S(1)} collective-permute-done((bf16[280,128]{1,0:T(8,128)(2,1)S(1)}, bf16[280,128]{1,0:T(8,128)(2,1)S(1)}, u32[]{:S(2)}, u32[]{:S(2)}) %collective-permute-start.1) | collective-permute-done | bytes 71712 | tf_op jit(solution)/shard_map/ppermute | solution.py:287
  12.6 1.2 %collective-permute-done.2 = bf16[280,128]{1,0:T(8,128)(2,1)S(1)} collective-permute-done((bf16[280,128]{1,0:T(8,128)(2,1)S(1)}, bf16[280,128]{1,0:T(8,128)(2,1)S(1)}, u32[]{:S(2)}, u32[]{:S(2)}) %collective-permute-start.2) | collective-permute-done | bytes 71712 | tf_op jit(solution)/shard_map/ppermute | solution.py:287
  13.8 0.1 collective-permute-start.3
  13.9 1.6 %collective-permute-start.5 = (bf16[4,24,128]{2,1,0:T(8,128)(2,1)S(1)}, bf16[4,24,128]{2,1,0:T(8,128)(2,1)S(1)}, u32[]{:S(2)}, u32[]{:S(2)}) collective-permute-start(bf16[4,24,128]{2,1,0:T(8,128)(2,1)S(1)} %slice.4), channel_id=1, source_target_pairs={{0,3},{1,2},{2,1},{3,0},{4,7},{5,6},{6,5},{7,4},{8,11},{9,10},{10,... | collective-permute-start | bytes 73736 | tf_op jit(solution)/shard_map/ppermute | solution.py:351
  15.5 0.5 %collective-permute-start.4 = (bf16[4,24,128]{2,1,0:T(8,128)(2,1)S(1)}, bf16[4,24,128]{2,1,0:T(8,128)(2,1)S(1)}, u32[]{:S(2)}, u32[]{:S(2)}) collective-permute-start(bf16[4,24,128]{2,1,0:T(8,128)(2,1)S(1)} %slice.4), channel_id=1, source_target_pairs={{0,2},{1,3},{2,0},{3,1},{4,6},{5,7},{6,4},{7,5},{8,10},{9,11},{10,... | collective-permute-start | bytes 73736 | tf_op jit(solution)/shard_map/ppermute | solution.py:351
  16.0 1.2 %shard_map.101 = (f32[1536,128]{1,0:T(8,128)S(1)}, bf16[8,128,128]{2,1,0:T(8,128)(2,1)S(1)}) custom-call(f32[1536,128]{1,0:T(8,128)} %constant.4.clone.row_source, bf16[8,128,128]{2,1,0:T(8,128)(2,1)} %constant.5.clone.column_source), custom_call_target="tpu_custom_call" | custom-call | bytes 2097152 | tf_op jit(solution)/shard_map/pallas_call | solution.py:365
  17.2 0.0 collective-permute-done.5.refs_3_
  17.2 2.1 %collective-permute-done.4.refs_2_ = bf16[4,24,128]{2,1,0:T(8,128)(2,1)S(1)} collective-permute-done((bf16[4,24,128]{2,1,0:T(8,128)(2,1)S(1)}, bf16[4,24,128]{2,1,0:T(8,128)(2,1)S(1)}, u32[]{:S(2)}, u32[]{:S(2)}) %collective-permute-start.4) | collective-permute-done | bytes 24608 | tf_op jit(solution)/shard_map/ppermute | solution.py:351
  19.3 0.0 collective-permute-done.3.refs_1_.refs_5_
  19.3 3.9 %shard_map.102 = f32[2,64,1024]{2,1,0:T(8,128)} custom-call(bf16[4,280,128]{2,1,0:T(8,128)(2,1)S(1)} %pad_maximum_fusion.refs_0_.refs_4_, bf16[4,280,128]{2,1,0:T(8,128)(2,1)S(1)} %collective-permute-done.3.refs_1_.refs_5_, bf16[4,24,128]{2,1,0:T(8,128)(2,1)S(1)} %collective-permute-done.4.refs_2_, bf16[4,24,128]{2,1,0:T(8,128)(2,1)S(1)} %collective-permute-done.5.refs_3_, ...), custom_call_target="tpu_custom_call" | custom-call | tf_op jit(solution)/shard_map/pallas_call | solution.py:375
  (2 shorter events, 0.0 us)
Async XLA Ops:
  1.8 5.7 %collective-permute-start = (bf16[280,128]{1,0:T(8,128)(2,1)S(1)}, bf16[280,128]{1,0:T(8,128)(2,1)S(1)}, u32[]{:S(2)}, u32[]{:S(2)}) collective-permute-start(bf16[280,128]{1,0:T(8,128)(2,1)S(1)} %get-tuple-element.12), channel_id=1, source_target_pairs={{0,4},{4,0},{8,12},{12,8},{1,5},{5,1},{9,13},{13,9},{2,6},{6,2},{1... | collective-permute-start | bytes 215048 | tf_op jit(solution)/shard_map/ppermute | solution.py:287
  4.9 7.7 %collective-permute-start.1 = (bf16[280,128]{1,0:T(8,128)(2,1)S(1)}, bf16[280,128]{1,0:T(8,128)(2,1)S(1)}, u32[]{:S(2)}, u32[]{:S(2)}) collective-permute-start(bf16[280,128]{1,0:T(8,128)(2,1)S(1)} %get-tuple-element.13), channel_id=1, source_target_pairs={{0,8},{4,12},{8,0},{12,4},{1,9},{5,13},{9,1},{13,5},{2,10},{6,14},... | collective-permute-start | bytes 215048 | tf_op jit(solution)/shard_map/ppermute | solution.py:287
  7.5 6.2 %collective-permute-start.2 = (bf16[280,128]{1,0:T(8,128)(2,1)S(1)}, bf16[280,128]{1,0:T(8,128)(2,1)S(1)}, u32[]{:S(2)}, u32[]{:S(2)}) collective-permute-start(bf16[280,128]{1,0:T(8,128)(2,1)S(1)} %get-tuple-element.14), channel_id=1, source_target_pairs={{0,12},{4,8},{8,4},{12,0},{1,13},{5,9},{9,5},{13,1},{2,14},{6,10},... | collective-permute-start | bytes 215048 | tf_op jit(solution)/shard_map/ppermute | solution.py:287
  13.8 5.5 %collective-permute-start.3 = (bf16[4,280,128]{2,1,0:T(8,128)(2,1)S(1)}, bf16[4,280,128]{2,1,0:T(8,128)(2,1)S(1)}, u32[]{:S(2)}, u32[]{:S(2)}) collective-permute-start(bf16[4,280,128]{2,1,0:T(8,128)(2,1)S(1)} %pad_maximum_fusion.refs_0_.refs_4_), channel_id=1, source_target_pairs={{0,1},{1,0},{2,3},{3,2},{4,5},{5,4},{6,7},{7,6},{8,9},{9,8},{10,11... | collective-permute-start | bytes 860168 | tf_op jit(solution)/shard_map/ppermute | solution.py:351
  13.9 3.3 %collective-permute-start.5 = (bf16[4,24,128]{2,1,0:T(8,128)(2,1)S(1)}, bf16[4,24,128]{2,1,0:T(8,128)(2,1)S(1)}, u32[]{:S(2)}, u32[]{:S(2)}) collective-permute-start(bf16[4,24,128]{2,1,0:T(8,128)(2,1)S(1)} %slice.4), channel_id=1, source_target_pairs={{0,3},{1,2},{2,1},{3,0},{4,7},{5,6},{6,5},{7,4},{8,11},{9,10},{10,... | collective-permute-start | bytes 73736 | tf_op jit(solution)/shard_map/ppermute | solution.py:351
  15.5 3.8 %collective-permute-start.4 = (bf16[4,24,128]{2,1,0:T(8,128)(2,1)S(1)}, bf16[4,24,128]{2,1,0:T(8,128)(2,1)S(1)}, u32[]{:S(2)}, u32[]{:S(2)}) collective-permute-start(bf16[4,24,128]{2,1,0:T(8,128)(2,1)S(1)} %slice.4), channel_id=1, source_target_pairs={{0,2},{1,3},{2,0},{3,1},{4,6},{5,7},{6,4},{7,5},{8,10},{9,11},{10,... | collective-permute-start | bytes 73736 | tf_op jit(solution)/shard_map/ppermute | solution.py:351
